TPU v7x, 512 devices: a whole 4x8x8 slice. The times are simulated.
512 devices in a mesh: ctx: 32 (over x, z_lo, core), head: 16 (over y, z_hi).
Axes of the slice: x: 4, y: 8, z: 8 (z_hi: 2, z_lo: 4; z = z_hi * 4 + z_lo), core: 2. Of those that a mesh axis runs over, the one named last changes fastest.
Arguments:
- queries: bfloat16 [4096, 8192], P('ctx', 'head'), may hold values from -9 to 9
- keys: bfloat16 [4096, 8192], P('ctx', 'head'), may hold values from -6 to 6
- values: bfloat16 [4096, 8192], P('ctx', 'head'), may hold values from -6 to 6
- d_out: bfloat16 [4096, 8192], P(('ctx', 'head')), may hold values from -6 to 6
- block_lists: int32 [32, 8], replicated, may hold values from 0 to 31, as said below
- list_counts: int32 [32], replicated, may hold values from 1 to 8, as said below
Outputs:
- attn_out: bfloat16 [4096, 8192], P('ctx', 'head')
- grad_q: bfloat16 [4096, 8192], P('ctx', 'head')
- grad_k: bfloat16 [4096, 8192], P('ctx', 'head')
- grad_v: bfloat16 [4096, 8192], P('ctx', 'head')
Inputs may be any that keep to these rules, and one draw needn't show every extreme that they name: `block_lists`: each row holds 8 distinct patch block ids; only the first list_counts entries of a row are read. Patch block p is held by index p of ctx. `list_counts`: some text block reads 8 patch blocks.
All inputs are finite; a program needn't handle non-finite values.
Results may differ from a plain program's by a relative error of at most 0.022.
Values may be sent and summed in bfloat16 or wider, within the bound.
A program may use at most 64 MiB of HBM per device.

v0:
```python
import math
import jax
import jax.numpy as jnp
from jax import lax
from jax.sharding import PartitionSpec as P

DH = 128
BLK = 128


def allowed_table(block_lists, list_counts, total_blocks):
    slot_ids = jnp.arange(block_lists.shape[1], dtype=jnp.int32)
    live_slots = slot_ids[None, :] < list_counts[:, None]
    block_ids = jnp.arange(total_blocks, dtype=jnp.int32)
    matches = (block_lists[:, :, None] == block_ids[None, None, :]) & live_slots[:, :, None]
    return jnp.any(matches, axis=1)


def tile_scores(query_rows, key_rows, scale):
    return (
        jnp.einsum("qhd,khd->hqk", query_rows, key_rows, preferred_element_type=jnp.float32) * scale
    )


def key_tile(heads_array, list_row, slot):
    return lax.dynamic_slice_in_dim(heads_array, list_row[slot] * BLK, BLK, 0)


def listed_forward(q_block, k_heads, v_heads, list_row, list_count, scale):
    heads = q_block.shape[1]

    def first_pass(slot, carry):
        running_max, running_total = carry
        scores = tile_scores(q_block, key_tile(k_heads, list_row, slot), scale)
        new_max = jnp.maximum(running_max, jnp.max(scores, axis=-1))
        running_total = running_total * jnp.exp(running_max - new_max) + jnp.sum(
            jnp.exp(scores - new_max[..., None]), axis=-1
        )
        return (new_max, running_total)

    start_max = jnp.full((heads, BLK), -jnp.inf, jnp.float32)
    start_total = jnp.zeros((heads, BLK), jnp.float32)
    row_max, row_total = lax.fori_loop(0, list_count, first_pass, (start_max, start_total))
    log_total = row_max + jnp.log(row_total)

    def second_pass(slot, acc):
        scores = tile_scores(q_block, key_tile(k_heads, list_row, slot), scale)
        weights = jnp.exp(scores - log_total[..., None]).astype(jnp.bfloat16)
        return acc + jnp.einsum(
            "hqk,khd->qhd",
            weights,
            key_tile(v_heads, list_row, slot),
            preferred_element_type=jnp.float32,
        )

    acc = lax.fori_loop(0, list_count, second_pass, jnp.zeros(q_block.shape, jnp.float32))
    return (log_total, acc.astype(jnp.bfloat16))


def listed_backward(
    q_block, d_block, k_heads, v_heads, list_row, list_count, log_total, row_delta, scale
):

    def tile_pass(slot, acc):
        key_rows = key_tile(k_heads, list_row, slot)
        scores = tile_scores(q_block, key_rows, scale)
        probs = jnp.exp(scores - log_total[..., None])
        dprobs = jnp.einsum(
            "qhd,khd->hqk",
            d_block,
            key_tile(v_heads, list_row, slot),
            preferred_element_type=jnp.float32,
        )
        dscores = (probs * (dprobs - row_delta[..., None])).astype(jnp.bfloat16)
        return acc + jnp.einsum(
            "hqk,khd->qhd", dscores, key_rows, preferred_element_type=jnp.float32
        )

    acc = lax.fori_loop(0, list_count, tile_pass, jnp.zeros(q_block.shape, jnp.float32))
    return (acc * scale).astype(jnp.bfloat16)


def shards(queries, keys, values, d_out, block_lists, list_counts):
    rows = queries.shape[0]
    heads = queries.shape[1] // DH
    scale = 1.0 / math.sqrt(DH)
    local_blocks = rows // BLK
    own_blocks = keys.shape[0] // BLK
    ctx_index = lax.axis_index("ctx")
    k_all, v_all = (
        lax.all_gather(keys, "ctx", axis=0, tiled=True),
        lax.all_gather(values, "ctx", axis=0, tiled=True),
    )
    total_blocks = k_all.shape[0] // BLK
    table = allowed_table(block_lists, list_counts, total_blocks)
    k_heads = k_all.reshape(-1, heads, DH)
    v_heads = v_all.reshape(-1, heads, DH)
    q_heads = queries.reshape(rows, heads, DH)
    d_rows = lax.all_to_all(d_out, "head", split_axis=1, concat_axis=0, tiled=True)
    d_heads = d_rows.reshape(rows, heads, DH)
    block = 0
    global_block = ctx_index * local_blocks + block
    list_row = lax.dynamic_index_in_dim(block_lists, global_block, 0, keepdims=False)
    list_count = lax.dynamic_index_in_dim(list_counts, global_block, 0, keepdims=False)
    log_block, out_block = listed_forward(q_heads, k_heads, v_heads, list_row, list_count, scale)
    delta_rows = jnp.sum(out_block.astype(jnp.float32) * d_heads.astype(jnp.float32), axis=-1).T
    block = 0
    global_block = ctx_index * local_blocks + block
    list_row = lax.dynamic_index_in_dim(block_lists, global_block, 0, keepdims=False)
    list_count = lax.dynamic_index_in_dim(list_counts, global_block, 0, keepdims=False)
    grads_list = listed_backward(
        q_heads, d_heads, k_heads, v_heads, list_row, list_count, log_block, delta_rows, scale
    )
    log_all, delta_all = (
        lax.all_gather(log_block, "ctx", axis=1, tiled=True),
        lax.all_gather(delta_rows, "ctx", axis=1, tiled=True),
    )
    own_table = lax.dynamic_slice_in_dim(table, ctx_index * own_blocks, own_blocks, 1)
    own_keys = jnp.repeat(own_table, BLK, axis=1).astype(jnp.float32)
    text_blocks = own_keys.shape[0]
    k_own = keys.reshape(-1, heads, DH)
    v_own = values.reshape(-1, heads, DH)
    d_piece = lax.all_gather(d_rows, "ctx", axis=0, tiled=True)
    count = d_piece.shape[0]
    row_block = jnp.arange(count, dtype=jnp.int32) // BLK
    one_hot = (row_block[:, None] == jnp.arange(text_blocks, dtype=jnp.int32)[None, :]).astype(
        jnp.float32
    )
    mask = jnp.dot(one_hot, own_keys) > 0.5
    q_three = lax.all_gather(queries, "ctx", axis=0, tiled=True).reshape(count, heads, DH)
    d_three = d_piece.reshape(count, heads, DH)
    scores = tile_scores(q_three, k_own, scale)
    probs = jnp.exp(jnp.where(mask[None], scores - log_all[..., None], -jnp.inf))
    weights = probs.astype(jnp.bfloat16)
    grad_values = jnp.einsum("hqk,qhd->khd", weights, d_three, preferred_element_type=jnp.float32)
    dprobs = jnp.einsum("qhd,khd->hqk", d_three, v_own, preferred_element_type=jnp.float32)
    dscores = (probs * (dprobs - delta_all[..., None])).astype(jnp.bfloat16)
    grad_keys = jnp.einsum("hqk,qhd->khd", dscores, q_three, preferred_element_type=jnp.float32)
    grad_keys, grad_values = (grad_keys, grad_values)
    attn_out = out_block.reshape(rows, heads * DH)
    grad_q = grads_list.reshape(rows, heads * DH)
    grad_k = (grad_keys * scale).astype(jnp.bfloat16).reshape(keys.shape)
    grad_v = grad_values.astype(jnp.bfloat16).reshape(values.shape)
    return (attn_out, grad_q, grad_k, grad_v)


def solution(mesh):
    return jax.shard_map(
        shards,
        mesh=mesh,
        in_specs=(
            P("ctx", "head"),
            P("ctx", "head"),
            P("ctx", "head"),
            P(("ctx", "head"), None),
            P(),
            P(),
        ),
        out_specs=(P("ctx", "head"), P("ctx", "head"), P("ctx", "head"), P("ctx", "head")),
        check_vma=False,
    )
```

profile of v0, /device:TPU:1, one launch (start us, length us, event | category | flops | bytes accessed | tf_op | source)
XLA Modules:
  0.0 357.4 jit_solution(11484293286546743806)
XLA Ops:
  7.2 1.7 copy.110
  8.9 1.7 copy.109
  10.7 1.7 copy.111
  12.4 28.8 %all_to_all.19 = bf16[8,16,512]{2,0,1:T(8,128)(2,1)} all-to-all(bf16[8,16,512]{2,0,1:T(8,128)(2,1)} %bitcast.89), channel_id=1, replica_groups=mesh['ctx'=32,'head'=16] {'head'}, dimensions={1} | all-to-all | bytes 262144 | tf_op jit(solution)/shard_map/all_to_all | solution.py:99
  41.2 0.8 copy.125
  42.0 0.9 dynamic-slice_reduce_fusion.1
  42.9 1.2 dynamic_slice.41
  44.1 1.0 copy.115
  45.1 0.7 iota_compare_fusion.3
  46.2 0.8 convolution_compare_fusion
  47.2 44.3 %all-gather.7.cloned.1.call-done = bf16[4096,512]{0,1:T(8,128)(2,1)} async-done(((bf16[128,512]{0,1:T(8,128)(2,1)}), bf16[4096,512]{0,1:T(8,128)(2,1)}) %all-gather.7.cloned.1.call-update) | async-done | bytes 4194320 | tf_op jit(solution)/shard_map/all_gather | solution.py:91
  91.5 6.3 %copy.114 = bf16[4096,4,128]{2,0,1:T(8,128)(2,1)} copy(bf16[4096,4,128]{0,2,1:T(8,128)(2,1)} %bitcast.76) | data formatting | bytes 8388608 | tf_op jit(solution)/shard_map/while | solution.py:56
  97.9 12.8 %while.32 = (s32[]{:T(128)}, f32[4,128]{1,0:T(4,128)S(1)}, f32[4,128]{1,0:T(4,128)S(1)}, s32[]{:T(128)}, s32[8]{0:T(128)S(1)}, /*index=5*/bf16[4096,4,128]{2,0,1...) while((s32[]{:T(128)}, f32[4,128]{1,0:T(4,128)S(1)}, ...), condition=%wide.region_3.4_spmd, body=%wide.region_0.3_spmd.sunk | while | flops 17040392 | bytes 813277 | solution.py:43
  98.5 0.6 dynamic_slice.73
  99.7 1.1 fusion.74
  101.5 0.6 dynamic_slice.73
  102.8 1.1 fusion.74
  104.6 0.6 dynamic_slice.73
  105.8 1.1 fusion.74
  107.6 0.6 dynamic_slice.73
  108.9 1.1 fusion.74
  110.7 57.2 %all-gather.5.cloned.1.call-done = bf16[4096,512]{0,1:T(8,128)(2,1)} async-done(((bf16[128,512]{0,1:T(8,128)(2,1)}), bf16[4096,512]{0,1:T(8,128)(2,1)}) %all-gather.5.cloned.1.call-update) | async-done | bytes 4194320 | tf_op jit(solution)/shard_map/all_gather | solution.py:92
  167.9 13.3 %while.33 = (s32[]{:T(128)}, f32[128,4,128]{0,2,1:T(8,128)S(1)}, s32[]{:T(128)}, s32[8]{0:T(128)S(1)}, bf16[4096,4,128]{0,2,1:T(8,128)(2,1)}, /*index=5*/bf16[40...) while((s32[]{:T(128)}, f32[128,4,128]{0,2,1:T(8,128)S(1)}, ...), condition=%wide.region_5.6_spmd, body=%wide.region_4.5_spmd.sunk | while | flops 33816584 | bytes 920801 | solution.py:56
  168.5 0.6 dynamic_slice.76
  169.7 1.4 fusion.78
  172.9 1.3 fusion.78
  176.1 1.4 fusion.78
  179.3 1.3 fusion.78
  181.3 0.8 copy.138
  182.3 18.1 %while.34 = (s32[]{:T(128)}, f32[128,4,128]{0,2,1:T(8,128)S(1)}, s32[]{:T(128)}, s32[8]{0:T(128)S(1)}, bf16[4096,4,128]{2,0,1:T(8,128)(2,1)}, /*index=5*/bf16[12...) while((s32[]{:T(128)}, f32[128,4,128]{0,2,1:T(8,128)S(1)}, ...), condition=%wide.region_8.9_spmd, body=%wide.region_7.8_spmd.sunk | while | flops 50724872 | bytes 1709301 | solution.py:79
  184.1 1.1 fusion.84
  185.3 1.4 fusion.85
  188.5 1.1 fusion.84
  189.6 1.4 fusion.85
  192.9 1.1 fusion.84
  194.0 1.4 fusion.85
  197.2 1.1 fusion.84
  198.4 1.4 fusion.85
  200.4 0.8 copy.139
  201.2 79.8 %all_gather.23 = f32[4,4096]{0,1:T(8,128)S(1)} all-gather(f32[4,128]{0,1:T(8,128)S(1)} %bitcast.83), channel_id=1, replica_groups=mesh['ctx'=32,'head'=16] {'ctx'}, dimensions={1}, use_global_device_ids=true | all-gather | bytes 67584 | tf_op jit(solution)/shard_map/all_gather | solution.py:116
  281.0 0.6 copy.132
  281.6 39.7 %all_gather.21 = f32[4,4096]{1,0:T(4,128)S(1)} all-gather(f32[4,128]{1,0:T(4,128)S(1)} %get-tuple-element.646), channel_id=1, replica_groups=mesh['ctx'=32,'head'=16] {'ctx'}, dimensions={1}, use_global_device_ids=true | all-gather | bytes 67584 | tf_op jit(solution)/shard_map/all_gather | solution.py:115
  321.3 7.8 %select_exponential_fusion = f32[4,4096,128]{2,1,0:T(8,128)} fusion(bf16[4096,4,128]{0,2,1:T(8,128)(2,1)} %bitcast.77, f32[4,4096]{1,0:T(4,128)S(1)} %all_gather.21, pred[4096,128]{1,0:T(8,128)(4,1)S(1)} %convolution_compare_fusion, bf16[128,512]{1,0:T(8,128)(2,1)S(1)} %copy-done.2), kind=kOutput, calls=%fused_computation.33 | convolution fusion | flops 543162368 | bytes 13303808 | tf_op jit(solution)/shard_map/qhd,khd->hqk/dot_general | solution.py:21
  329.1 6.5 %copy.129 = bf16[4096,512]{0,1:T(8,128)(2,1)} copy(bf16[4096,512]{1,0:T(8,128)(2,1)} %all-gather.11.cloned.1.call-done) | data formatting | bytes 8388608 | tf_op jit(solution)/shard_map/all_gather | solution.py:123
  335.5 5.9 %fusion.33 = bf16[4,128,128]{1,2,0:T(8,128)(2,1)S(1)} fusion(bf16[4096,4,128]{0,2,1:T(8,128)(2,1)} %bitcast.74, f32[4,4096,128]{2,1,0:T(8,128)} %select_exponential_fusion), kind=kOutput, calls=%fused_computation.40 | convolution fusion | flops 539033600 | bytes 12713984 | tf_op jit(solution)/shard_map/hqk,qhd->khd/dot_general | solution.py:135
  341.5 7.9 %fusion.32 = bf16[4,128,128]{1,2,0:T(8,128)(2,1)S(1)} fusion(bf16[4096,4,128]{0,2,1:T(8,128)(2,1)} %bitcast.78, f32[4,4096,128]{2,1,0:T(8,128)} %select_exponential_fusion, bf16[4096,4,128]{0,2,1:T(8,128)(2,1)} %bitcast.75, f32[4,4096]{1,0:T(4,128)S(1)} %copy.132, bf16[128,512]{1,0:T(8,128)(2,1)S(1)} %copy-done.1), kind=kOutput, calls=%fused_computation.39 | convolution fusion | flops 1080164352 | bytes 17104896 | tf_op jit(solution)/shard_map/hqk,qhd->khd/dot_general | solution.py:138
  349.4 0.8 copy.134
  350.1 0.8 copy.133
  (54 shorter events, 5.5 us)
Async XLA Ops:
  7.2 84.3 %all-gather.7.cloned.1.call-start = ((), (), s32[]{:S(2)}) async-start(), calls=%async_computation.2 | async-start | bytes 4325376 | tf_op jit(solution)/shard_map/all_gather | solution.py:91
  8.9 159.0 %all-gather.5.cloned.1.call-start = ((), (), s32[]{:S(2)}) async-start(), calls=%async_computation.1 | async-start | bytes 4325376 | tf_op jit(solution)/shard_map/all_gather | solution.py:92
  10.6 310.6 %all-gather.9.cloned.1.call-start = ((), (), s32[]{:S(2)}) async-start(), calls=%async_computation.3 | async-start | bytes 4325376 | tf_op jit(solution)/shard_map/all_gather | solution.py:130
  12.4 316.7 %all-gather.11.cloned.1.call-start = ((), (), s32[]{:S(2)}) async-start(), calls=%async_computation.4 | async-start | bytes 4325376 | tf_op jit(solution)/shard_map/all_gather | solution.py:123
  41.2 5.8 %copy-start = (bf16[8,16,512]{2,0,1:T(8,128)(2,1)S(1)}, bf16[8,16,512]{2,0,1:T(8,128)(2,1)}, u32[]{:S(2)}) copy-start(bf16[8,16,512]{2,0,1:T(8,128)(2,1)} %all_to_all.19) | copy-start | bytes 393220
  200.3 120.9 %copy-start.2 = (bf16[128,512]{1,0:T(8,128)(2,1)S(1)}, bf16[128,512]{1,0:T(8,128)(2,1)}, u32[]{:S(2)}) copy-start(bf16[128,512]{1,0:T(8,128)(2,1)} %param.13) | copy-start | bytes 393220
  335.5 5.9 %copy-start.1 = (bf16[128,512]{1,0:T(8,128)(2,1)S(1)}, bf16[128,512]{1,0:T(8,128)(2,1)}, u32[]{:S(2)}) copy-start(bf16[128,512]{1,0:T(8,128)(2,1)} %param.14) | copy-start | bytes 393220
Sparse Core Ops, SparseCore 0:
  10.6 80.8 all-gather.6
  94.1 73.7 all-gather.4
  170.5 74.7 all-gather.8
  247.3 66.9 all-gather.10
where the time goes:
time: 359 us; the launch traced here: 357 us
  blocking collectives  148 us (41%)
  waiting for transfers between devices  102 us (28%)
  matrix products  42.4 us (12%)
  local copies, waits for them, and re-layouts  33.1 us (9%)
  loops' own time  16.8 us (5%)
  between operations  13.9 us (4%)
    all_gather x1, blocking collectives, shards(): lax.all_gather(delta_rows, 'ctx', axis=1, tiled=True)  79.8 us
    all_gather x1, waiting for transfers between devices, shards(): lax.all_gather(values, 'ctx', axis=0, tiled=True)  57.2 us
    all_gather x1, waiting for transfers between devices, shards(): lax.all_gather(keys, 'ctx', axis=0, tiled=True)  44.3 us
    all_gather x1, blocking collectives, shards(): lax.all_gather(log_block, 'ctx', axis=1, tiled=True)  39.7 us
    all_to_all x1, blocking collectives, shards(): lax.all_to_all(d_out, 'head', split_axis=1, concat_axis=0, tiled=True)  28.8 us
    dot_general x9, matrix products, tile_scores(): jnp.einsum('qhd,khd->hqk', query_rows, key_rows, preferred_element_type=j...  16.9 us
    dot_general x1, matrix products, shards(): jnp.einsum('hqk,qhd->khd', dscores, q_three, preferred_element_type=jnp.f...  7.87 us
    unnamed x13, local copies, waits for them, and re-layouts  7.46 us
  transfers between devices with their start and end apart: 4, of which 2 were waited for; matrix products, arithmetic and copies ran while one was open for 15% of the time, Pallas kernels for 0%

commit v1 on v0

--- a/solution.py
+++ b/solution.py
@@ -112,7 +112,9 @@
         q_heads, d_heads, k_heads, v_heads, list_row, list_count, log_block, delta_rows, scale
     )
     log_all, delta_all = (
-        lax.all_gather(log_block, "ctx", axis=1, tiled=True),
+        jnp.concatenate(
+            lax.all_to_all(jnp.stack([log_block] * lax.axis_size("ctx")), "ctx", 0, 0), axis=1
+        ),
         lax.all_gather(delta_rows, "ctx", axis=1, tiled=True),
     )
     own_table = lax.dynamic_slice_in_dim(table, ctx_index * own_blocks, own_blocks, 1)

time: 359 us -> 346 us (0.964)
  blocking collectives: 148 us -> 111 us
  starting transfers between devices: 0.16 us -> 16.5 us
  waiting for transfers between devices: 102 us -> 107 us
    all_gather x1 -> x0, blocking collectives: 39.7 us -> none  [shards(): lax.all_gather(log_block, 'ctx', axis=1, tiled=True)]
    all_gather x1, waiting for transfers between devices: 0.01 us -> 21.5 us  [shards(): d_piece = lax.all_gather(d_rows, 'ctx', axis=0, tiled=True)]
    all_to_all x0 -> x1, starting transfers between devices: none -> 16.4 us  [shards(): lax.all_to_all(jnp.stack([log_block] * lax.axis_size('ctx')), 'ctx', 0, 0)]
    all_gather x1, waiting for transfers between devices: 57.2 us -> 41.2 us  [shards(): lax.all_gather(values, 'ctx', axis=0, tiled=True)]
  transfers between devices with their start and end apart: 4 -> 5, of which waited for: 2 -> 3; matrix products, arithmetic and copies ran while one was open for 15% -> 16% of each run, Pallas kernels for 0% -> 0%
where the time goes in v1:
time: 346 us; the launch traced here: 344 us
  blocking collectives  111 us (32%)
  waiting for transfers between devices  107 us (31%)
  matrix products  42.5 us (12%)
  local copies, waits for them, and re-layouts  33.8 us (10%)
  loops' own time  18.3 us (5%)
  starting transfers between devices  16.5 us (5%)
  between operations  13.9 us (4%)
    all_gather x1, blocking collectives, shards(): lax.all_gather(delta_rows, 'ctx', axis=1, tiled=True)  82.3 us
    all_gather x1, waiting for transfers between devices, shards(): lax.all_gather(keys, 'ctx', axis=0, tiled=True)  44.2 us
    all_gather x1, waiting for transfers between devices, shards(): lax.all_gather(values, 'ctx', axis=0, tiled=True)  41.2 us
    all_to_all x1, blocking collectives, shards(): lax.all_to_all(d_out, 'head', split_axis=1, concat_axis=0, tiled=True)  28.8 us
    all_gather x1, waiting for transfers between devices, shards(): d_piece = lax.all_gather(d_rows, 'ctx', axis=0, tiled=True)  21.5 us
    dot_general x9, matrix products, tile_scores(): jnp.einsum('qhd,khd->hqk', query_rows, key_rows, preferred_element_type=j...  17 us
    all_to_all x1, starting transfers between devices, shards(): lax.all_to_all(jnp.stack([log_block] * lax.axis_size('ctx')), 'ctx', 0, 0)  16.4 us
    dot_general x1, matrix products, shards(): jnp.einsum('hqk,qhd->khd', dscores, q_three, preferred_element_type=jnp.f...  7.87 us
  transfers between devices with their start and end apart: 5, of which 3 were waited for; matrix products, arithmetic and copies ran while one was open for 16% of the time, Pallas kernels for 0%

profile of v1, /device:TPU:1, one launch (start us, length us, event | category | flops | bytes accessed | tf_op | source)
XLA Modules:
  0.0 344.4 jit_solution(12786631848269061400)
XLA Ops:
  7.2 1.7 copy.110
  8.9 1.7 copy.109
  10.7 1.7 copy.111
  12.4 28.8 %all_to_all.24 = bf16[8,16,512]{2,0,1:T(8,128)(2,1)} all-to-all(bf16[8,16,512]{2,0,1:T(8,128)(2,1)} %bitcast.92), channel_id=1, replica_groups=mesh['ctx'=32,'head'=16] {'head'}, dimensions={1} | all-to-all | bytes 262144 | tf_op jit(solution)/shard_map/all_to_all | solution.py:99
  41.2 0.8 copy.125
  42.0 0.9 dynamic-slice_reduce_fusion.1
  42.9 1.3 dynamic_slice.41
  44.2 1.0 copy.115
  45.2 0.7 iota_compare_fusion.3
  46.3 0.8 convolution_compare_fusion
  47.3 44.2 %all-gather.7.cloned.1.call-done = bf16[4096,512]{0,1:T(8,128)(2,1)} async-done(((bf16[128,512]{0,1:T(8,128)(2,1)}), bf16[4096,512]{0,1:T(8,128)(2,1)}) %all-gather.7.cloned.1.call-update) | async-done | bytes 4194320 | tf_op jit(solution)/shard_map/all_gather | solution.py:91
  91.5 6.4 %copy.114 = bf16[4096,4,128]{2,0,1:T(8,128)(2,1)} copy(bf16[4096,4,128]{0,2,1:T(8,128)(2,1)} %bitcast.79) | data formatting | bytes 8388608 | tf_op jit(solution)/shard_map/while | solution.py:56
  97.9 13.3 %while.32 = (s32[]{:T(128)}, f32[4,128]{1,0:T(4,128)S(1)}, f32[4,128]{1,0:T(4,128)S(1)}, s32[]{:T(128)}, s32[8]{0:T(128)S(1)}, /*index=5*/bf16[4096,4,128]{2,0,1...) while((s32[]{:T(128)}, f32[4,128]{1,0:T(4,128)S(1)}, ...), condition=%wide.region_3.4_spmd, body=%wide.region_0.3_spmd.sunk | while | flops 17040392 | bytes 813277 | solution.py:43
  98.6 0.6 dynamic_slice.73
  99.8 1.1 fusion.74
  101.7 0.6 dynamic_slice.73
  103.0 1.1 fusion.74
  104.9 0.6 dynamic_slice.73
  106.1 1.1 fusion.74
  109.3 1.1 fusion.74
  111.2 0.6 stack.2
  111.9 16.4 %all-to-all-start.1 = ((f32[32,4,128]{2,1,0:T(4,128)}), f32[32,4,128]{2,1,0:T(4,128)S(1)}, u32[]{:S(2)}, u32[]{:S(2)}) async-start(f32[32,4,128]{2,1,0:T(4,128)} %stack.2), calls=%async_computation.1 | async-start | bytes 131072 | tf_op jit(solution)/shard_map/all_to_all | solution.py:116
  128.2 41.2 %all-gather.5.cloned.1.call-done = bf16[4096,512]{0,1:T(8,128)(2,1)} async-done(((bf16[128,512]{0,1:T(8,128)(2,1)}), bf16[4096,512]{0,1:T(8,128)(2,1)}) %all-gather.5.cloned.1.call-update) | async-done | bytes 4194320 | tf_op jit(solution)/shard_map/all_gather | solution.py:92
  169.5 13.8 %while.33 = (s32[]{:T(128)}, f32[128,4,128]{0,2,1:T(8,128)S(1)}, s32[]{:T(128)}, s32[8]{0:T(128)S(1)}, bf16[4096,4,128]{0,2,1:T(8,128)(2,1)}, /*index=5*/bf16[40...) while((s32[]{:T(128)}, f32[128,4,128]{0,2,1:T(8,128)S(1)}, ...), condition=%wide.region_5.6_spmd, body=%wide.region_4.5_spmd.sunk | while | flops 33816584 | bytes 920801 | solution.py:56
  171.4 1.4 fusion.78
  174.7 1.3 fusion.78
  178.0 1.4 fusion.78
  181.3 1.3 fusion.78
  183.6 18.6 %while.34 = (s32[]{:T(128)}, f32[128,4,128]{0,2,1:T(8,128)S(1)}, s32[]{:T(128)}, s32[8]{0:T(128)S(1)}, bf16[4096,4,128]{2,0,1:T(8,128)(2,1)}, /*index=5*/bf16[12...) while((s32[]{:T(128)}, f32[128,4,128]{0,2,1:T(8,128)S(1)}, ...), condition=%wide.region_8.9_spmd, body=%wide.region_7.8_spmd.sunk | while | flops 50724872 | bytes 1709301 | solution.py:79
  185.5 1.1 fusion.84
  186.6 1.4 fusion.85
  190.0 1.1 fusion.84
  191.1 1.4 fusion.85
  194.4 1.1 fusion.84
  195.6 1.4 fusion.85
  198.9 1.1 fusion.84
  200.1 1.4 fusion.85
  202.2 0.8 copy.138
  203.0 0.8 copy.139
  203.7 82.3 %all_gather.19 = f32[4,4096]{0,1:T(8,128)S(1)} all-gather(f32[4,128]{0,1:T(8,128)S(1)} %bitcast.86), channel_id=1, replica_groups=mesh['ctx'=32,'head'=16] {'ctx'}, dimensions={1}, use_global_device_ids=true | all-gather | bytes 67584 | tf_op jit(solution)/shard_map/all_gather | solution.py:118
  286.0 0.6 copy.132
  286.7 7.9 %select_exponential_fusion = f32[4,4096,128]{2,1,0:T(8,128)} fusion(bf16[4096,4,128]{0,2,1:T(8,128)(2,1)} %bitcast.80, f32[4,4096]{1,0:T(4,128)S(1)} %bitcast.93, pred[4096,128]{1,0:T(8,128)(4,1)S(1)} %convolution_compare_fusion, bf16[128,512]{1,0:T(8,128)(2,1)S(1)} %copy-done.2), kind=kOutput, calls=%fused_computation.33 | convolution fusion | flops 543162368 | bytes 13303808 | tf_op jit(solution)/shard_map/qhd,khd->hqk/dot_general | solution.py:21
  294.6 21.5 %all-gather.11.cloned.1.call-done = bf16[4096,512]{1,0:T(8,128)(2,1)} async-done(((bf16[128,512]{1,0:T(8,128)(2,1)}), bf16[4096,512]{1,0:T(8,128)(2,1)}) %all-gather.11.cloned.1.call-update) | async-done | bytes 4194320 | tf_op jit(solution)/shard_map/all_gather | solution.py:125
  316.1 6.4 %copy.129 = bf16[4096,512]{0,1:T(8,128)(2,1)} copy(bf16[4096,512]{1,0:T(8,128)(2,1)} %all-gather.11.cloned.1.call-done) | data formatting | bytes 8388608 | tf_op jit(solution)/shard_map/all_gather | solution.py:125
  322.5 5.9 %fusion.33 = bf16[4,128,128]{1,2,0:T(8,128)(2,1)S(1)} fusion(bf16[4096,4,128]{0,2,1:T(8,128)(2,1)} %bitcast.77, f32[4,4096,128]{2,1,0:T(8,128)} %select_exponential_fusion), kind=kOutput, calls=%fused_computation.40 | convolution fusion | flops 539033600 | bytes 12713984 | tf_op jit(solution)/shard_map/hqk,qhd->khd/dot_general | solution.py:137
  328.4 7.9 %fusion.32 = bf16[4,128,128]{1,2,0:T(8,128)(2,1)S(1)} fusion(bf16[4096,4,128]{0,2,1:T(8,128)(2,1)} %bitcast.81, f32[4,4096,128]{2,1,0:T(8,128)} %select_exponential_fusion, bf16[4096,4,128]{0,2,1:T(8,128)(2,1)} %bitcast.78, f32[4,4096]{1,0:T(4,128)S(1)} %copy.132, bf16[128,512]{1,0:T(8,128)(2,1)S(1)} %copy-done.1), kind=kOutput, calls=%fused_computation.39 | convolution fusion | flops 1080164352 | bytes 17104896 | tf_op jit(solution)/shard_map/hqk,qhd->khd/dot_general | solution.py:140
  336.3 0.8 copy.134
  337.1 0.8 copy.133
  (56 shorter events, 6.7 us)
Async XLA Ops:
  7.2 84.4 %all-gather.7.cloned.1.call-start = ((), (), s32[]{:S(2)}) async-start(), calls=%async_computation.3 | async-start | bytes 4325376 | tf_op jit(solution)/shard_map/all_gather | solution.py:91
  8.9 160.5 %all-gather.5.cloned.1.call-start = ((), (), s32[]{:S(2)}) async-start(), calls=%async_computation.2 | async-start | bytes 4325376 | tf_op jit(solution)/shard_map/all_gather | solution.py:92
  10.6 276.0 %all-gather.9.cloned.1.call-start = ((), (), s32[]{:S(2)}) async-start(), calls=%async_computation.4 | async-start | bytes 4325376 | tf_op jit(solution)/shard_map/all_gather | solution.py:132
  12.4 303.7 %all-gather.11.cloned.1.call-start = ((), (), s32[]{:S(2)}) async-start(), calls=%async_computation.5 | async-start | bytes 4325376 | tf_op jit(solution)/shard_map/all_gather | solution.py:125
  41.2 5.9 %copy-start = (bf16[8,16,512]{2,0,1:T(8,128)(2,1)S(1)}, bf16[8,16,512]{2,0,1:T(8,128)(2,1)}, u32[]{:S(2)}) copy-start(bf16[8,16,512]{2,0,1:T(8,128)(2,1)} %all_to_all.24) | copy-start | bytes 393220
  111.9 174.8 %all-to-all-start.1 = ((f32[32,4,128]{2,1,0:T(4,128)}), f32[32,4,128]{2,1,0:T(4,128)S(1)}, u32[]{:S(2)}, u32[]{:S(2)}) async-start(f32[32,4,128]{2,1,0:T(4,128)} %stack.2), calls=%async_computation.1 | async-start | bytes 131072 | tf_op jit(solution)/shard_map/all_to_all | solution.py:116
  202.1 84.5 %copy-start.2 = (bf16[128,512]{1,0:T(8,128)(2,1)S(1)}, bf16[128,512]{1,0:T(8,128)(2,1)}, u32[]{:S(2)}) copy-start(bf16[128,512]{1,0:T(8,128)(2,1)} %param.13) | copy-start | bytes 393220
  322.5 5.9 %copy-start.1 = (bf16[128,512]{1,0:T(8,128)(2,1)S(1)}, bf16[128,512]{1,0:T(8,128)(2,1)}, u32[]{:S(2)}) copy-start(bf16[128,512]{1,0:T(8,128)(2,1)} %param.14) | copy-start | bytes 393220
Sparse Core Ops, SparseCore 0:
  10.6 80.8 all-gather.6
  94.1 75.2 all-gather.4
  172.1 73.1 all-gather.8
  247.3 68.7 all-gather.10
